TPU v7x, 32 devices: a whole 2x2x4 slice. The times are simulated.
32 devices in a mesh: ens: 2 (over y), space: 4 (over z), tm: 2 (over x), mom: 2 (over core).
Axes of the slice: x: 2, y: 2, z: 4, core: 2. Of those that a mesh axis runs over, the one named last changes fastest.
Arguments:
- eigvecs: bfloat16 [8, 2, 3, 256, 2048], P(('ens', 'tm'), None, None, None, 'space'), parts along dimension 0, may hold values from -0.359375 to 0.359375
- momenta: int32 [4, 3], P('mom'), may hold values from 1 to 2
- pairs: int32 [2, 2], replicated, may hold values from 0 to 3, as said below
- spin_weights: float32 [4, 4], replicated, may hold values from -1 to 1
- perambulators: bfloat16 [4, 2, 4, 4, 256, 256], P(('ens', 'tm'), None, None, None, 'space'), parts along dimension 0, may hold values from -0.0234375 to 0.0234375
Outputs:
- blocks: bfloat16 [4, 4, 2, 256, 256], P(('ens', 'tm'), 'mom', None, 'space'), parts along dimension 0
There are 2 independent parts, one for each index of `ens`. A program takes and returns all parts, laid end to end along the dimension named above; an argument that names none is the same for every part. Nothing has to cross between parts.
Inputs may be any that keep to these rules, and one draw needn't show every extreme that they name: pairs[q, 0], the sink, lies in time group q: (q) * 2 <= pairs[q, 0] < (q + 1) * 2; pairs[q, 1], the source, is any timeslice.
All inputs are finite; a program needn't handle non-finite values.
Results may differ from a plain program's by a relative error of at most 0.008.
Values may be sent and summed in bfloat16 or wider, within the bound.
No kernel may reach another device: no remote copies, remote signals or barrier semaphores. Data moves between devices by JAX's collectives and lax.ppermute only.
A program may use at most 64 MiB of HBM per device.

v0:
```python
import math
import jax
import jax.numpy as jnp
from jax import lax
from jax.sharding import PartitionSpec as P

LAT = 48
EXACT_PRECISION = lax.Precision.HIGHEST


def phases(momenta, site_ids):
    xcoord = (site_ids % LAT).astype(jnp.float32)
    ycoord = (site_ids // LAT % LAT).astype(jnp.float32)
    zcoord = (site_ids // (LAT * LAT)).astype(jnp.float32)
    mom_float = momenta.astype(jnp.float32)
    angles = (
        mom_float[:, 0:1] * xcoord + mom_float[:, 1:2] * ycoord + mom_float[:, 2:3] * zcoord
    ) * (2.0 * math.pi / LAT)
    return (jnp.cos(angles), jnp.sin(angles))


def elemental_terms(eigvecs, cosine_rows, sine_rows):
    contract_dims = (((0, 2), (0, 2)), ((), ()))
    per_time = []
    for which_time in range(eigvecs.shape[0]):
        real_vec = eigvecs[which_time, 0]
        imag_vec = eigvecs[which_time, 1]
        real_wide = real_vec.astype(jnp.float32)
        imag_wide = imag_vec.astype(jnp.float32)
        per_mom = []
        for which_mom in range(cosine_rows.shape[0]):
            cosine = cosine_rows[which_mom]
            sine = sine_rows[which_mom]
            real_turned = (cosine * real_wide + sine * imag_wide).astype(jnp.bfloat16)
            imag_turned = (cosine * imag_wide - sine * real_wide).astype(jnp.bfloat16)
            real_part = lax.dot_general(
                real_vec, real_turned, contract_dims, preferred_element_type=jnp.float32
            ) + lax.dot_general(
                imag_vec, imag_turned, contract_dims, preferred_element_type=jnp.float32
            )
            imag_part = lax.dot_general(
                real_vec, imag_turned, contract_dims, preferred_element_type=jnp.float32
            ) - lax.dot_general(
                imag_vec, real_turned, contract_dims, preferred_element_type=jnp.float32
            )
            per_mom.append(jnp.stack([real_part, imag_part]))
        per_time.append(jnp.stack(per_mom))
    return jnp.stack(per_time)


def source_slots(held_rows, pairs, my_group, times_dev, tm_size, pair_dev):
    wanted = pairs[:, 1].reshape(tm_size, pair_dev)
    local_times = jnp.arange(times_dev, dtype=jnp.int32) + my_group * times_dev
    chosen = (wanted[:, :, None] == local_times).astype(jnp.bfloat16)
    return jnp.einsum(
        "rqt,tmcij->rqmcij", chosen, held_rows, preferred_element_type=jnp.float32
    ).astype(jnp.bfloat16)


def sink_select(held_rows, my_pairs, my_group, times_dev):
    local_times = jnp.arange(times_dev, dtype=jnp.int32) + my_group * times_dev
    chosen = (my_pairs[:, 0][:, None] == local_times).astype(jnp.bfloat16)
    return jnp.einsum(
        "qt,tmcij->qmcij", chosen, held_rows, preferred_element_type=jnp.float32
    ).astype(jnp.bfloat16)


def bridge(mixed_block, source):
    real_part = jnp.einsum(
        "qkl,qmjl->qmkj", mixed_block[:, 0], source[:, :, 0], preferred_element_type=jnp.float32
    ) + jnp.einsum(
        "qkl,qmjl->qmkj", mixed_block[:, 1], source[:, :, 1], preferred_element_type=jnp.float32
    )
    imag_part = jnp.einsum(
        "qkl,qmjl->qmkj", mixed_block[:, 1], source[:, :, 0], preferred_element_type=jnp.float32
    ) - jnp.einsum(
        "qkl,qmjl->qmkj", mixed_block[:, 0], source[:, :, 1], preferred_element_type=jnp.float32
    )
    return jnp.stack([real_part, imag_part], 2).astype(jnp.bfloat16)


def attach(sink_elem, bridged):
    real_part = jnp.einsum(
        "qmik,qmkj->qmij", sink_elem[:, :, 0], bridged[:, :, 0], preferred_element_type=jnp.float32
    ) - jnp.einsum(
        "qmik,qmkj->qmij", sink_elem[:, :, 1], bridged[:, :, 1], preferred_element_type=jnp.float32
    )
    imag_part = jnp.einsum(
        "qmik,qmkj->qmij", sink_elem[:, :, 0], bridged[:, :, 1], preferred_element_type=jnp.float32
    ) + jnp.einsum(
        "qmik,qmkj->qmij", sink_elem[:, :, 1], bridged[:, :, 0], preferred_element_type=jnp.float32
    )
    return jnp.stack([real_part, imag_part], 2)


def local(eigvecs, momenta, pairs, spin_weights, perambulators):
    times_dev = eigvecs.shape[0]
    vec_count = eigvecs.shape[3]
    sites_dev = eigvecs.shape[4]
    pair_dev = perambulators.shape[0]
    tm_size = lax.axis_size("tm")
    space_size = lax.axis_size("space")
    my_group = lax.axis_index("tm")
    my_place = lax.axis_index("space")
    rows_dev = vec_count // space_size
    row_first = my_place * rows_dev
    site_ids = my_place * sites_dev + jnp.arange(sites_dev, dtype=jnp.int32)
    cosine_rows, sine_rows = phases(momenta, site_ids)
    partial_value = elemental_terms(eigvecs, cosine_rows, sine_rows)
    my_pairs = lax.dynamic_slice_in_dim(pairs, my_group * pair_dev, pair_dev, 0)
    whole = lax.psum(partial_value, "space").astype(jnp.bfloat16)
    outgoing = source_slots(whole, pairs, my_group, times_dev, tm_size, pair_dev)
    arrived = lax.all_to_all(outgoing, "tm", split_axis=0, concat_axis=0, tiled=True)
    source_full = jnp.sum(arrived, axis=0, dtype=jnp.float32).astype(jnp.bfloat16)
    sink_whole = sink_select(whole, my_pairs, my_group, times_dev)
    sink_own = lax.dynamic_slice_in_dim(sink_whole, row_first, rows_dev, 3)
    mixed_peramb = jnp.einsum(
        "ab,qcabkl->qckl",
        spin_weights,
        perambulators.astype(jnp.float32),
        precision=EXACT_PRECISION,
    ).astype(jnp.bfloat16)
    bridged = bridge(lax.all_gather(mixed_peramb, "space", axis=2, tiled=True), source_full)
    blocks = attach(sink_own, bridged).astype(jnp.bfloat16)
    return blocks


def solution(mesh):
    return jax.shard_map(
        local,
        mesh=mesh,
        in_specs=(
            P(("ens", "tm"), None, None, None, "space"),
            P("mom", None),
            P(),
            P(),
            P(("ens", "tm"), None, None, None, "space", None),
        ),
        out_specs=P(("ens", "tm"), "mom", None, "space", None),
        check_vma=False,
    )
```

profile of v0, /device:TPU:0, one launch (start us, length us, event | category | flops | bytes accessed | tf_op | source)
XLA Modules:
  0.0 120.1 jit_solution(8111220607492806430)
XLA Ops:
  0.0 0.8 convert_element_type.166
  1.3 2.2 %convolution_bitcast_fusion.14 = f32[256,256]{1,0:T(8,128)S(1)} fusion(f32[512]{0:T(512)S(1)} %bitcast.288, f32[512]{0:T(512)S(1)} %bitcast.296, bf16[2,2,3,256,512]{4,3,2,1,0:T(8,128)(2,1)} %param.5), kind=kOutput, calls=%fused_computation.55 | convolution fusion | flops 203685888 | bytes 2625536 | tf_op jit(solution)/shard_map/dot_general | solution.py:38
  3.5 0.4 copy-done.1
  3.9 0.4 convolution_bitcast_fusion.12
  4.3 0.5 convolution_bitcast_fusion.10
  4.8 0.4 convolution_bitcast_fusion.8
  5.2 0.4 convolution_bitcast_fusion.6
  5.7 0.5 convolution_bitcast_fusion.4
  6.1 0.5 convolution_bitcast_fusion.2
  6.6 0.4 convolution_bitcast_fusion
  7.1 0.4 fusion.22
  7.5 0.5 fusion.24
  8.0 0.5 fusion.26
  8.4 0.5 fusion.28
  8.9 0.5 fusion.30
  9.4 0.5 fusion.32
  9.8 0.5 fusion.34
  10.3 0.5 fusion.36
  11.2 79.3 %all-reduce.1 = bf16[2,2,2,256,256]{3,4,2,1,0:T(8,128)(2,1)} all-reduce(f32[2,2,2,256,256]{3,4,2,1,0:T(8,128)S(1)} %pad_maximum_fusion), channel_id=1, replica_groups=mesh['ens'=2,'space'=4,'tm'=2,'mom'=2] {'space'}, use_global_device_ids=true, to_apply=%region_0.1 | all-reduce | flops 524288 | bytes 3145728 | tf_op jit(solution)/shard_map/psum | solution.py:111
  90.5 2.5 %copy.12 = bf16[2,2,2,256,256]{4,0,3,2,1:T(2,128)(2,1)S(1)} copy(bf16[2,2,2,256,256]{3,4,2,1,0:T(8,128)(2,1)} %all-reduce.1) | data formatting | bytes 2097152 | tf_op jit(solution)/shard_map/convert_element_type | solution.py:111
  93.3 1.3 %fusion.16 = bf16[2,1,2,2,256,256]{5,0,4,3,2,1:T(2,128)(2,1)S(1)} fusion(bf16[2,2,2,256,256]{4,0,3,2,1:T(2,128)(2,1)S(1)} %copy.12, s32[2]{0:T(128)S(1)} %iota_add_fusion.1, s32[2]{0:T(128)S(1)} %slice_reduce_fusion), kind=kOutput, calls=%fused_computation.34 | convolution fusion | flops 2621444 | bytes 2097168 | tf_op jit(solution)/shard_map/rqt,tmcij->rqmcij/dot_general | solution.py:55
  94.6 1.1 copy.13
  95.7 3.9 %all-to-all-start = ((bf16[2,1,2,2,256,256]{5,4,3,2,1,0:T(8,128)(2,1)}), bf16[2,1,2,2,256,256]{5,4,3,2,1,0:T(8,128)(2,1)S(1)}, u32[]{:S(2)}, u32[]{:S(2)}) async-start(bf16[2,1,2,2,256,256]{5,4,3,2,1,0:T(8,128)(2,1)} %copy.13), calls=%async_computation | async-start | bytes 2097152 | tf_op jit(solution)/shard_map/all_to_all | solution.py:113
  99.6 2.1 %fusion.41 = bf16[1,2,64,256,1]{3,0,4,2,1:T(2,128)(2,1)S(1)} fusion(f32[4,4,1,1,1]{1,2,0,4,3:T(1,128)S(1)} %bitcast.304, bf16[2,4,4,64,256]{4,3,2,1,0:T(8,128)(2,1)S(1)} %bitcast.261), kind=kOutput, calls=%fused_computation.82 | convolution fusion | flops 6291456 | bytes 1114176 | tf_op jit(solution)/shard_map/ab,qcabkl->qckl/dot_general | solution.py:117
  101.8 1.3 %fusion.145 = bf16[1,2,2,256,256]{4,0,3,2,1:T(2,128)(2,1)S(1)} fusion(bf16[2,2,2,256,256]{4,0,3,2,1:T(2,128)(2,1)S(1)} %copy.12, s32[]{:T(128)S(1)} %bitcast.305, s32[]{:T(128)S(6)} %mul.205), kind=kOutput, calls=%fused_computation.194 | convolution fusion | flops 1048580 | bytes 1572872 | tf_op jit(solution)/shard_map/qt,tmcij->qmcij/dot_general | solution.py:63
  103.1 13.8 %all-gather = bf16[2,256,256]{2,1,0:T(8,128)(2,1)S(1)} all-gather(bf16[2,64,256]{2,1,0:T(8,128)(2,1)S(1)} %bitcast.271), channel_id=2, replica_groups=mesh['ens'=2,'space'=4,'tm'=2,'mom'=2] {'space'}, dimensions={1}, use_global_device_ids=true | all-gather | bytes 327680 | tf_op jit(solution)/shard_map/all_gather | solution.py:123
  116.9 0.5 reduce_sum.14
  117.5 0.2 fusion.100
  117.7 0.3 fusion.99
  118.0 0.3 fusion.20
  118.3 0.3 fusion.19
  119.4 0.7 copy.20
  (34 shorter events, 2.1 us)
Async XLA Ops:
  0.0 99.6 %copy-start = (bf16[1,2,4,4,64,256]{5,4,3,2,1,0:T(8,128)(2,1)S(1)}, bf16[1,2,4,4,64,256]{5,4,3,2,1,0:T(8,128)(2,1)}, u32[]{:S(2)}) copy-start(bf16[1,2,4,4,64,256]{5,4,3,2,1,0:T(8,128)(2,1)} %param.9) | copy-start | bytes 3145732
  1.3 2.6 %copy-start.1 = (bf16[2,2,3,256,512]{4,3,2,1,0:T(8,128)(2,1)S(1)}, bf16[2,2,3,256,512]{4,3,2,1,0:T(8,128)(2,1)}, u32[]{:S(2)}) copy-start(bf16[2,2,3,256,512]{4,3,2,1,0:T(8,128)(2,1)} %param.5) | copy-start | bytes 9437188
  90.5 2.6 %copy-start.3 = (s32[2,2]{1,0:T(2,128)S(1)}, s32[2,2]{1,0:T(2,128)}, u32[]{:S(2)}) copy-start(s32[2,2]{1,0:T(2,128)} %param.7) | copy-start | bytes 52
  95.7 3.9 %copy-start.2 = (f32[4,4]{1,0:T(4,128)S(1)}, f32[4,4]{1,0:T(4,128)}, u32[]{:S(2)}) copy-start(f32[4,4]{1,0:T(4,128)} %param.8) | copy-start | bytes 196
  95.7 21.2 %all-to-all-start = ((bf16[2,1,2,2,256,256]{5,4,3,2,1,0:T(8,128)(2,1)}), bf16[2,1,2,2,256,256]{5,4,3,2,1,0:T(8,128)(2,1)S(1)}, u32[]{:S(2)}, u32[]{:S(2)}) async-start(bf16[2,1,2,2,256,256]{5,4,3,2,1,0:T(8,128)(2,1)} %copy.13), calls=%async_computation | async-start | bytes 2097152 | tf_op jit(solution)/shard_map/all_to_all | solution.py:113
where the time goes:
time: 120 us
  blocking collectives  93.1 us (78%)
  matrix products  15.5 us (13%)
  local copies, waits for them, and re-layouts  5.32 us (4%)
  starting transfers between devices  3.89 us (3%)
  other arithmetic  1.86 us (2%)
    psum x1, blocking collectives, local(): whole = lax.psum(partial_value, 'space').astype(jnp.bfloat16)  79.3 us
    all_gather x1, blocking collectives, local(): lax.all_gather(mixed_peramb, 'space', axis=2, tiled=True)  13.8 us
    all_to_all x1, starting transfers between devices, local(): lax.all_to_all(outgoing, 'tm', split_axis=0, concat_axis=0, tiled=True)  3.89 us
    dot_general x4, matrix products, elemental_terms(): lax.dot_general(imag_vec, imag_turned, contract_dims, preferred_element_t...  3.57 us
    convert_element_type x1, local copies, waits for them, and re-layouts, local(): whole = lax.psum(partial_value, 'space').astype(jnp.bfloat16)  2.54 us
  transfers between devices with their start and end apart: 1, of which 0 were waited for; matrix products, arithmetic and copies ran while one was open for 3% of the time, Pallas kernels for 0%

commit v1 on v0

--- a/solution.py
+++ b/solution.py
@@ -1,3 +1,4 @@
+import functools
 import math
 import jax
 import jax.numpy as jnp
@@ -6,6 +7,19 @@
 
 LAT = 48
 EXACT_PRECISION = lax.Precision.HIGHEST
+
+
+def _link_zones(in_array, dimension_no):
+    n_lanes = jax.lax.psum(1, "space")
+    trail = [n_lanes if j == dimension_no else 1 for j in range(in_array.ndim)]
+    local_next = jnp.tile(in_array, trail)
+    carry_in = jax.lax.all_to_all(
+        local_next, "space", concat_axis=dimension_no, tiled=True, split_axis=dimension_no
+    )
+    return carry_in
+
+
+write_spans = functools.partial(_link_zones, dimension_no=2)
 
 
 def phases(momenta, site_ids):
@@ -120,7 +134,7 @@
         perambulators.astype(jnp.float32),
         precision=EXACT_PRECISION,
     ).astype(jnp.bfloat16)
-    bridged = bridge(lax.all_gather(mixed_peramb, "space", axis=2, tiled=True), source_full)
+    bridged = bridge(write_spans(mixed_peramb), source_full)
     blocks = attach(sink_own, bridged).astype(jnp.bfloat16)
     return blocks
 

time: 120 us -> 121 us (level)
  blocking collectives: 93.1 us -> 77 us
  waiting for transfers between devices: 0.01 us -> 8.18 us
  starting transfers between devices: 3.89 us -> 9.94 us
  local copies, waits for them, and re-layouts: 5.32 us -> 7.86 us
    all_gather x1 -> x0, blocking collectives: 13.8 us -> none  [local(): lax.all_gather(mixed_peramb, 'space', axis=2, tiled=True)]
    all_to_all x1, waiting for transfers between devices: 0.01 us -> 8.17 us  [local(): lax.all_to_all(outgoing, 'tm', split_axis=0, concat_axis=0, tiled=True)]
    all_to_all x0 -> x1, starting transfers between devices: none -> 6.35 us  [_link_zones(): jax.lax.all_to_all(local_next, 'space', concat_axis=dimension_no, tiled=T...]
    psum x1, blocking collectives: 79.3 us -> 77 us  [local(): whole = lax.psum(partial_value, 'space').astype(jnp.bfloat16)]
    unnamed x8, local copies, waits for them, and re-layouts: 0.38 us -> 1.6 us
  transfers between devices with their start and end apart: 1 -> 2, of which waited for: 0 -> 1; matrix products, arithmetic and copies ran while one was open for 3% -> 14% of each run, Pallas kernels for 0% -> 0%
where the time goes in v1:
time: 121 us
  blocking collectives  77 us (64%)
  matrix products  16.2 us (13%)
  starting transfers between devices  9.94 us (8%)
  waiting for transfers between devices  8.18 us (7%)
  local copies, waits for them, and re-layouts  7.86 us (6%)
    psum x1, blocking collectives, local(): whole = lax.psum(partial_value, 'space').astype(jnp.bfloat16)  77 us
    all_to_all x1, waiting for transfers between devices, local(): lax.all_to_all(outgoing, 'tm', split_axis=0, concat_axis=0, tiled=True)  8.17 us
    all_to_all x1, starting transfers between devices, _link_zones(): jax.lax.all_to_all(local_next, 'space', concat_axis=dimension_no, tiled=T...  6.35 us
    all_to_all x1, starting transfers between devices, local(): lax.all_to_all(outgoing, 'tm', split_axis=0, concat_axis=0, tiled=True)  3.59 us
    dot_general x4, matrix products, elemental_terms(): lax.dot_general(imag_vec, imag_turned, contract_dims, preferred_element_t...  3.57 us
    dot_general x1, matrix products, local(): jnp.einsum('ab,qcabkl->qckl', spin_weights, perambulators.astype(jnp.floa...  2.8 us
    convert_element_type x1, local copies, waits for them, and re-layouts, local(): whole = lax.psum(partial_value, 'space').astype(jnp.bfloat16)  2.54 us
  transfers between devices with their start and end apart: 2, of which 1 were waited for; matrix products, arithmetic and copies ran while one was open for 14% of the time, Pallas kernels for 0%

profile of v1, /device:TPU:0, one launch (start us, length us, event | category | flops | bytes accessed | tf_op | source)
XLA Modules:
  0.0 120.7 jit_solution(16919143586066798621)
XLA Ops:
  0.0 1.2 %copy-done = bf16[1,2,4,4,64,256]{5,4,3,2,1,0:T(8,128)(2,1)S(1)} copy-done((bf16[1,2,4,4,64,256]{5,4,3,2,1,0:T(8,128)(2,1)S(1)}, bf16[1,2,4,4,64,256]{5,4,3,2,1,0:T(8,128)(2,1)}, u32[]{:S(2)}) %copy-start) | copy-done | bytes 1048600
  1.2 2.8 %fusion.41 = bf16[1,2,64,256,1]{3,0,4,2,1:T(2,128)(2,1)S(1)} fusion(f32[4,4,1,1,1]{1,2,0,4,3:T(1,128)} %bitcast.300, bf16[2,4,4,64,256]{4,3,2,1,0:T(8,128)(2,1)S(1)} %bitcast.261), kind=kOutput, calls=%fused_computation.82 | convolution fusion | flops 6291456 | bytes 1114176 | tf_op jit(solution)/shard_map/ab,qcabkl->qckl/dot_general | solution.py:131
  4.1 0.9 tile.4
  5.0 6.3 %all-to-all-start.1 = ((bf16[1,2,256,256]{3,1,0,2:T(2,128)(2,1)}), bf16[1,2,256,256]{3,1,0,2:T(2,128)(2,1)S(1)}, u32[]{:S(2)}, u32[]{:S(2)}) async-start(bf16[1,2,256,256]{3,1,0,2:T(2,128)(2,1)} %bitcast.69), calls=%async_computation.1 | async-start | bytes 524288 | tf_op jit(solution)/shard_map/all_to_all | solution.py:16
  11.9 2.2 %convolution_bitcast_fusion.14 = f32[256,256]{1,0:T(8,128)S(1)} fusion(f32[512]{0:T(512)S(1)} %bitcast.284, f32[512]{0:T(512)S(1)} %bitcast.292, bf16[2,2,3,256,512]{4,3,2,1,0:T(8,128)(2,1)} %param.5), kind=kOutput, calls=%fused_computation.55 | convolution fusion | flops 203685888 | bytes 2625536 | tf_op jit(solution)/shard_map/dot_general | solution.py:52
  14.1 0.4 copy-done.2
  14.5 0.4 convolution_bitcast_fusion.12
  14.9 0.5 convolution_bitcast_fusion.10
  15.4 0.4 convolution_bitcast_fusion.8
  15.8 0.5 convolution_bitcast_fusion.6
  16.3 0.5 convolution_bitcast_fusion.4
  16.7 0.5 convolution_bitcast_fusion.2
  17.2 0.4 convolution_bitcast_fusion
  17.7 0.4 fusion.22
  18.1 0.5 fusion.24
  18.6 0.5 fusion.26
  19.0 0.5 fusion.28
  19.5 0.5 fusion.30
  20.0 0.5 fusion.32
  20.4 0.5 fusion.34
  20.9 0.5 fusion.36
  21.8 77.0 %all-reduce.1 = bf16[2,2,2,256,256]{3,4,2,1,0:T(8,128)(2,1)} all-reduce(f32[2,2,2,256,256]{3,4,2,1,0:T(8,128)S(1)} %pad_maximum_fusion), channel_id=1, replica_groups=mesh['ens'=2,'space'=4,'tm'=2,'mom'=2] {'space'}, use_global_device_ids=true, to_apply=%region_0.1 | all-reduce | flops 524288 | bytes 3145728 | tf_op jit(solution)/shard_map/psum | solution.py:125
  99.0 2.5 %copy.12 = bf16[2,2,2,256,256]{4,0,3,2,1:T(2,128)(2,1)S(1)} copy(bf16[2,2,2,256,256]{3,4,2,1,0:T(8,128)(2,1)} %all-reduce.1) | data formatting | bytes 2097152 | tf_op jit(solution)/shard_map/convert_element_type | solution.py:125
  101.6 1.3 %fusion.16 = bf16[2,1,2,2,256,256]{5,0,4,3,2,1:T(2,128)(2,1)S(1)} fusion(bf16[2,2,2,256,256]{4,0,3,2,1:T(2,128)(2,1)S(1)} %copy.12, s32[2]{0:T(128)S(1)} %iota_add_fusion.1, s32[2]{0:T(128)S(1)} %slice_reduce_fusion), kind=kOutput, calls=%fused_computation.34 | convolution fusion | flops 2621444 | bytes 2097168 | tf_op jit(solution)/shard_map/rqt,tmcij->rqmcij/dot_general | solution.py:69
  102.9 1.1 copy.13
  104.0 3.6 %all-to-all-start = ((bf16[2,1,2,2,256,256]{5,4,3,2,1,0:T(8,128)(2,1)}), bf16[2,1,2,2,256,256]{5,4,3,2,1,0:T(8,128)(2,1)S(1)}, u32[]{:S(2)}, u32[]{:S(2)}) async-start(bf16[2,1,2,2,256,256]{5,4,3,2,1,0:T(8,128)(2,1)} %copy.13), calls=%async_computation | async-start | bytes 2097152 | tf_op jit(solution)/shard_map/all_to_all | solution.py:127
  107.6 1.3 %fusion.145 = bf16[1,2,2,256,256]{4,0,3,2,1:T(2,128)(2,1)S(1)} fusion(bf16[2,2,2,256,256]{4,0,3,2,1:T(2,128)(2,1)S(1)} %copy.12, s32[]{:T(128)S(1)} %bitcast.301, s32[]{:T(128)S(6)} %mul.205), kind=kOutput, calls=%fused_computation.194 | convolution fusion | flops 1048580 | bytes 1572872 | tf_op jit(solution)/shard_map/qt,tmcij->qmcij/dot_general | solution.py:77
  109.0 0.4 fusion.150
  109.4 8.2 %all-to-all-done = bf16[2,1,2,2,256,256]{5,4,3,2,1,0:T(8,128)(2,1)S(1)} async-done(((bf16[2,1,2,2,256,256]{5,4,3,2,1,0:T(8,128)(2,1)}), bf16[2,1,2,2,256,256]{5,4,3,2,1,0:T(8,128)(2,1)S(1)}, u32[]{:S(2)}, u32[]{:S(2)}) %all-to-all-start) | async-done | bytes 1048608 | tf_op jit(solution)/shard_map/all_to_all | solution.py:127
  117.6 0.5 reduce_sum.14
  118.9 0.3 fusion.19
  120.0 0.7 copy.22
  (37 shorter events, 3.0 us)
Async XLA Ops:
  0.0 1.2 %copy-start = (bf16[1,2,4,4,64,256]{5,4,3,2,1,0:T(8,128)(2,1)S(1)}, bf16[1,2,4,4,64,256]{5,4,3,2,1,0:T(8,128)(2,1)}, u32[]{:S(2)}) copy-start(bf16[1,2,4,4,64,256]{5,4,3,2,1,0:T(8,128)(2,1)} %param.9) | copy-start | bytes 3145732
  1.2 10.2 %copy-start.1 = (s32[2,3]{1,0:T(2,128)S(1)}, s32[2,3]{1,0:T(2,128)}, u32[]{:S(2)}) copy-start(s32[2,3]{1,0:T(2,128)} %param.6) | copy-start | bytes 76
  5.0 99.0 %all-to-all-start.1 = ((bf16[1,2,256,256]{3,1,0,2:T(2,128)(2,1)}), bf16[1,2,256,256]{3,1,0,2:T(2,128)(2,1)S(1)}, u32[]{:S(2)}, u32[]{:S(2)}) async-start(bf16[1,2,256,256]{3,1,0,2:T(2,128)(2,1)} %bitcast.69), calls=%async_computation.1 | async-start | bytes 524288 | tf_op jit(solution)/shard_map/all_to_all | solution.py:16
  11.9 2.6 %copy-start.2 = (bf16[2,2,3,256,512]{4,3,2,1,0:T(8,128)(2,1)S(1)}, bf16[2,2,3,256,512]{4,3,2,1,0:T(8,128)(2,1)}, u32[]{:S(2)}) copy-start(bf16[2,2,3,256,512]{4,3,2,1,0:T(8,128)(2,1)} %param.5) | copy-start | bytes 9437188
  21.8 77.0 %copy-start.3 = (s32[2,2]{1,0:T(2,128)S(1)}, s32[2,2]{1,0:T(2,128)}, u32[]{:S(2)}) copy-start(s32[2,2]{1,0:T(2,128)} %param.7) | copy-start | bytes 52
  104.0 13.5 %all-to-all-start = ((bf16[2,1,2,2,256,256]{5,4,3,2,1,0:T(8,128)(2,1)}), bf16[2,1,2,2,256,256]{5,4,3,2,1,0:T(8,128)(2,1)S(1)}, u32[]{:S(2)}, u32[]{:S(2)}) async-start(bf16[2,1,2,2,256,256]{5,4,3,2,1,0:T(8,128)(2,1)} %copy.13), calls=%async_computation | async-start | bytes 2097152 | tf_op jit(solution)/shard_map/all_to_all | solution.py:127
